TPU v7x, 32 devices: a whole 2x2x4 slice. The times are simulated.
32 devices in a mesh: segment: 4 (over z), mp: 4 (over y, core), tok: 2 (over x).
Axes of the slice: x: 2, y: 2, z: 4, core: 2. Of those that a mesh axis runs over, the one named last changes fastest.
Arguments:
- weights_in: bfloat16 [4, 2, 512, 32768], P('segment', None, None, 'mp'), may hold values from -0.25 to 0.25
- weights_out: bfloat16 [4, 2, 32768, 512], P('segment', None, 'mp'), may hold values from -0.03125 to 0.03125
- norm_gains: float32 [4, 2, 512], P('segment'), may hold values from 0.5 to 1.5
- activations: bfloat16 [4, 2, 2, 256, 512], P('segment', None, 'tok', 'mp'), may hold values from -6 to 6
- gradients: bfloat16 [4, 2, 2, 256, 512], P('segment', None, 'tok', 'mp'), may hold values from -6 to 6
- fresh_inputs: bfloat16 [1, 2, 256, 512], P(None, 'tok', 'mp'), may hold values from -6 to 6
- fresh_gradients: bfloat16 [1, 2, 256, 512], P(None, 'tok', 'mp'), may hold values from -6 to 6
- stashed_inputs: bfloat16 [2, 4, 2, 2, 256, 512], P(None, 'segment', None, 'tok', 'mp'), may hold values from -6 to 6
- stashed_preact: bfloat16 [2, 4, 2, 2, 256, 32768], P(None, 'segment', None, 'tok', None, 'mp'), may hold values from -6 to 6
Outputs:
- leaving_acts: bfloat16 [2, 4, 2, 2, 256, 512], P(None, 'segment', None, 'tok', 'mp')
- leaving_grads: bfloat16 [2, 4, 2, 2, 256, 512], P(None, 'segment', None, 'tok', 'mp')
All inputs are finite; a program needn't handle non-finite values.
Results may differ from a plain program's by a relative error of at most 0.014.
Values may be sent and summed in bfloat16 or wider, within the bound.
A program may use at most 128 MiB of HBM per device.

v0:
```python
import jax
import jax.numpy as jnp
from jax import lax
from jax.sharding import PartitionSpec as P

TICKS = 2


epsilon = 1e-06
contract_last = (((1,), (1,)), ((), ()))


def from_behind(value, axis, steps):
    count = lax.axis_size(axis)
    leading, last = (max(0, -steps), min(count, count - steps))
    return lax.ppermute(value, axis, [(source, source + steps) for source in range(leading, last)])


def normalize(values, gain_row):
    values_wide = values.astype(jnp.float32)
    inverse = lax.rsqrt(jnp.mean(values_wide * values_wide, axis=-1, keepdims=True) + epsilon)
    return values_wide * inverse * gain_row


def norm_backward(gradient, stashed, gain_row, norm_grad):
    stashed_wide = stashed.astype(jnp.float32)
    inverse = lax.rsqrt(jnp.mean(stashed_wide * stashed_wide, axis=-1, keepdims=True) + epsilon)
    scaled = gain_row * norm_grad
    inner_sum = jnp.mean(stashed_wide * scaled, axis=-1, keepdims=True)
    result = (
        gradient.astype(jnp.float32)
        + inverse * scaled
        - stashed_wide * inverse * inverse * inverse * inner_sum
    )
    return result.astype(jnp.bfloat16)


def forward_term(normed_rows, weight_in, weight_out):
    hidden = jax.nn.relu(
        jnp.dot(normed_rows, weight_in, preferred_element_type=jnp.float32)
    ).astype(jnp.bfloat16)
    return jnp.dot(hidden, weight_out, preferred_element_type=jnp.float32)


def backward_term(grad_rows, stash_pre, weight_in, weight_out):
    upward = lax.dot_general(
        grad_rows, weight_out, contract_last, preferred_element_type=jnp.float32
    )
    masked = jnp.where(stash_pre > 0, upward, jnp.zeros_like(upward)).astype(jnp.bfloat16)
    return lax.dot_general(masked, weight_in, contract_last, preferred_element_type=jnp.float32)


def send_later(out_down, back_up):
    return from_behind((out_down, back_up), "segment", 1)


def send_earlier(out_up, back_down):
    return from_behind((out_up, back_down), "segment", -1)


def body(
    weights_in,
    weights_out,
    norm_gains,
    activations,
    gradients,
    fresh_inputs,
    fresh_gradients,
    stashed_inputs,
    stashed_preact,
):
    segment_index = lax.axis_index("segment")
    is_first = segment_index == 0
    is_last = segment_index == lax.axis_size("segment") - 1
    feature_count = activations.shape[-1]
    acts_now = activations[0, :, 0]
    grads_now = gradients[0, :, 0]
    leaving_forward = []
    leaving_backward = []
    for tick_index in range(TICKS):
        more_ticks = tick_index + 1 < TICKS
        normed = jnp.stack(
            [normalize(acts_now[leg_index], norm_gains[0, leg_index]) for leg_index in range(2)]
        ).astype(jnp.bfloat16)
        gathered, grad_rows = (
            lax.all_gather(normed, "mp", axis=1, tiled=True),
            lax.all_gather(grads_now, "mp", axis=1, tiled=True),
        )
        stash_pre = stashed_preact[tick_index, 0, :, 0]
        stashed = stashed_inputs[tick_index, 0, :, 0]

        def finish_forward(leg_index, totals):
            return (acts_now[leg_index].astype(jnp.float32) + totals).astype(jnp.bfloat16)

        def finish_backward(leg_index, totals):
            return norm_backward(
                grads_now[leg_index], stashed[leg_index], norm_gains[0, leg_index], totals
            )

        stacked = lax.psum_scatter(
            jnp.concatenate(
                [
                    forward_term(gathered[0], weights_in[0, 0], weights_out[0, 0]),
                    forward_term(gathered[1], weights_in[0, 1], weights_out[0, 1]),
                    backward_term(grad_rows[0], stash_pre[0], weights_in[0, 0], weights_out[0, 0]),
                    backward_term(grad_rows[1], stash_pre[1], weights_in[0, 1], weights_out[0, 1]),
                ],
                axis=1,
            ).astype(jnp.bfloat16),
            "mp",
            scatter_dimension=0,
            tiled=True,
        ).astype(jnp.float32)
        out_down = finish_forward(0, stacked[:, :feature_count])
        out_up = finish_forward(1, stacked[:, feature_count : 2 * feature_count])
        back_down = finish_backward(0, stacked[:, 2 * feature_count : 3 * feature_count])
        back_up = finish_backward(1, stacked[:, 3 * feature_count :])
        if more_ticks:
            from_lower = send_later(out_down, back_up)
            from_upper = send_earlier(out_up, back_down)
        leaving_forward.append(jnp.stack([out_down, out_up]))
        leaving_backward.append(jnp.stack([back_down, back_up]))
        if more_ticks:
            acts_now = jnp.stack(
                [
                    jnp.where(is_first, fresh_inputs[tick_index, 0], from_lower[0]),
                    jnp.where(is_last, out_down, from_upper[0]),
                ]
            )
            grads_now = jnp.stack(
                [
                    jnp.where(is_last, back_up, from_upper[1]),
                    jnp.where(is_first, fresh_gradients[tick_index, 0], from_lower[1]),
                ]
            )
    leaving_acts = jnp.stack(leaving_forward)[:, None, :, None]
    leaving_grads = jnp.stack(leaving_backward)[:, None, :, None]
    return (leaving_acts, leaving_grads)


def solution(mesh):
    return jax.shard_map(
        body,
        mesh=mesh,
        in_specs=(
            P("segment", None, None, "mp"),
            P("segment", None, "mp", None),
            P("segment", None, None),
            P("segment", None, "tok", "mp", None),
            P("segment", None, "tok", "mp", None),
            P(None, "tok", "mp", None),
            P(None, "tok", "mp", None),
            P(None, "segment", None, "tok", "mp", None),
            P(None, "segment", None, "tok", None, "mp"),
        ),
        out_specs=(
            P(None, "segment", None, "tok", "mp", None),
            P(None, "segment", None, "tok", "mp", None),
        ),
        check_vma=False,
    )
```

profile of v0, /device:TPU:0, one launch (start us, length us, event | category | flops | bytes accessed | tf_op | source)
XLA Modules:
  0.0 201.6 jit_solution(7215292975198119959)
XLA Ops:
  7.2 0.8 fusion.176
  8.0 1.0 fusion.108
  9.0 1.0 fusion.112
  10.0 8.7 %all_gather.12 = bf16[2,256,512]{2,1,0:T(8,128)(2,1)S(1)} all-gather(bf16[2,64,512]{2,1,0:T(8,128)(2,1)S(1)} %pad_maximum_fusion.2), channel_id=1, replica_groups=mesh['segment'=4,'mp'=4,'tok'=2] {'mp'}, dimensions={1}, use_global_device_ids=true | all-gather | bytes 655360 | tf_op jit(solution)/shard_map/all_gather | solution.py:86
  18.7 10.4 %fusion.64 = bf16[256,512]{1,0:T(8,128)(2,1)S(1)} fusion(bf16[1,2,8192,512]{3,2,1,0:T(8,128)(2,1)} %param.10, bf16[1,2,512,8192]{3,2,1,0:T(8,128)(2,1)} %param.9, bf16[2,256,512]{2,1,0:T(8,128)(2,1)S(1)} %all_gather.12), kind=kOutput, calls=%fused_computation.56 | convolution fusion | flops 4299292672 | bytes 17301504 | tf_op jit(solution)/shard_map/dot_general | solution.py:42
  29.1 10.4 %fusion.74 = bf16[256,512]{1,0:T(8,128)(2,1)S(1)} fusion(bf16[1,2,8192,512]{3,2,1,0:T(8,128)(2,1)} %param.10, bf16[1,2,512,8192]{3,2,1,0:T(8,128)(2,1)} %param.9, bf16[2,256,512]{2,1,0:T(8,128)(2,1)S(1)} %all_gather.12), kind=kOutput, calls=%fused_computation.58 | convolution fusion | flops 4299292672 | bytes 17301504 | tf_op jit(solution)/shard_map/dot_general | solution.py:42
  39.5 7.5 %all-gather = bf16[1,2,1,256,512]{4,3,2,1,0:T(8,128)(2,1)S(1)} all-gather(bf16[1,2,1,64,512]{4,3,2,1,0:T(8,128)(2,1)S(1)} %copy-done.2), channel_id=2, replica_groups=mesh['segment'=4,'mp'=4,'tok'=2] {'mp'}, dimensions={3}, use_global_device_ids=true | all-gather | bytes 655360 | tf_op jit(solution)/shard_map/all_gather | solution.py:87
  47.0 9.4 %fusion.84 = bf16[256,512]{1,0:T(8,128)(2,1)S(1)} fusion(bf16[1,2,512,8192]{3,2,1,0:T(8,128)(2,1)} %param.9, bf16[1,2,8192,512]{3,2,1,0:T(8,128)(2,1)} %param.10, bf16[2,1,2,1,256,8192]{5,4,3,2,1,0:T(8,128)(2,1)} %param.17, bf16[1,2,1,256,512]{4,3,2,1,0:T(8,128)(2,1)S(1)} %all-gather), kind=kOutput, calls=%fused_computation.60 | convolution fusion | flops 4301389824 | bytes 21495808 | tf_op jit(solution)/shard_map/dot_general | solution.py:50
  56.5 9.5 %fusion.94 = bf16[256,512]{1,0:T(8,128)(2,1)S(1)} fusion(bf16[1,2,512,8192]{3,2,1,0:T(8,128)(2,1)} %param.9, bf16[1,2,8192,512]{3,2,1,0:T(8,128)(2,1)} %param.10, bf16[2,1,2,1,256,8192]{5,4,3,2,1,0:T(8,128)(2,1)} %param.17, bf16[1,2,1,256,512]{4,3,2,1,0:T(8,128)(2,1)S(1)} %all-gather), kind=kOutput, calls=%fused_computation.62 | convolution fusion | flops 4301389824 | bytes 21495808 | tf_op jit(solution)/shard_map/dot_general | solution.py:50
  66.0 1.1 pad_maximum_fusion
  67.2 25.7 %reduce-scatter.3.cloned.1.call-done = bf16[64,2048]{1,0:T(8,128)(2,1)} async-done(((bf16[256,2048]{1,0:T(8,128)(2,1)}), bf16[64,2048]{1,0:T(8,128)(2,1)}) %reduce-scatter.3.cloned.1.call-update) | async-done | bytes 262160 | tf_op jit(solution)/shard_map/reduce_scatter | solution.py:100
  92.9 1.0 convert_element_type.158
  93.9 1.3 collective-permute-start.1
  95.2 4.9 %collective-permute-done.1 = bf16[64,512]{1,0:T(8,128)(2,1)S(1)} collective-permute-done((bf16[64,512]{1,0:T(8,128)(2,1)S(1)}, bf16[64,512]{1,0:T(8,128)(2,1)S(1)}, u32[]{:S(2)}, u32[]{:S(2)}) %collective-permute-start.1) | collective-permute-done | bytes 65568 | tf_op jit(solution)/shard_map/ppermute | solution.py:16
  100.1 0.2 fusion.122
  100.3 3.4 %collective-permute-start = (bf16[64,512]{1,0:T(8,128)(2,1)S(1)}, bf16[64,512]{1,0:T(8,128)(2,1)S(1)}, u32[]{:S(2)}, u32[]{:S(2)}) collective-permute-start(bf16[64,512]{1,0:T(8,128)(2,1)S(1)} %get-tuple-element.18), channel_id=1, source_target_pairs={{0,8},{8,16},{16,24},{1,9},{9,17},{17,25},{2,10},{10,18},{18,26},{... | collective-permute-start | bytes 196616 | tf_op jit(solution)/shard_map/ppermute | solution.py:16
  103.8 1.8 collective-permute-done
  105.9 6.5 %all_gather.14 = bf16[2,256,512]{2,1,0:T(8,128)(2,1)S(1)} all-gather(bf16[2,64,512]{2,1,0:T(8,128)(2,1)S(1)} %pad_maximum_fusion.3), channel_id=1, replica_groups=mesh['segment'=4,'mp'=4,'tok'=2] {'mp'}, dimensions={1}, use_global_device_ids=true | all-gather | bytes 655360 | tf_op jit(solution)/shard_map/all_gather | solution.py:86
  112.4 1.3 collective-permute-start.2
  113.7 10.4 %fusion.69 = bf16[256,512]{1,0:T(8,128)(2,1)S(1)} fusion(bf16[1,2,8192,512]{3,2,1,0:T(8,128)(2,1)} %param.10, bf16[1,2,512,8192]{3,2,1,0:T(8,128)(2,1)} %param.9, bf16[2,256,512]{2,1,0:T(8,128)(2,1)S(1)} %all_gather.14), kind=kOutput, calls=%fused_computation.57 | convolution fusion | flops 4299292672 | bytes 17301504 | tf_op jit(solution)/shard_map/dot_general | solution.py:42
  124.2 5.2 %collective-permute-start.3 = (bf16[64,512]{1,0:T(8,128)(2,1)S(1)}, bf16[64,512]{1,0:T(8,128)(2,1)S(1)}, u32[]{:S(2)}, u32[]{:S(2)}) collective-permute-start(bf16[64,512]{1,0:T(8,128)(2,1)S(1)} %get-tuple-element.20), channel_id=1, source_target_pairs={{0,8},{8,16},{16,24},{1,9},{9,17},{17,25},{2,10},{10,18},{18,26},{... | collective-permute-start | bytes 196616 | tf_op jit(solution)/shard_map/ppermute | solution.py:16
  129.5 10.4 %fusion.79 = bf16[256,512]{1,0:T(8,128)(2,1)S(1)} fusion(bf16[1,2,8192,512]{3,2,1,0:T(8,128)(2,1)} %param.10, bf16[1,2,512,8192]{3,2,1,0:T(8,128)(2,1)} %param.9, bf16[2,256,512]{2,1,0:T(8,128)(2,1)S(1)} %all_gather.14), kind=kOutput, calls=%fused_computation.59 | convolution fusion | flops 4299292672 | bytes 17301504 | tf_op jit(solution)/shard_map/dot_general | solution.py:42
  139.9 7.0 %all_gather.15 = bf16[2,256,512]{2,1,0:T(8,128)(2,1)S(1)} all-gather(bf16[2,64,512]{2,1,0:T(8,128)(2,1)S(1)} %pad_maximum_fusion.4), channel_id=1, replica_groups=mesh['segment'=4,'mp'=4,'tok'=2] {'mp'}, dimensions={1}, use_global_device_ids=true | all-gather | bytes 655360 | tf_op jit(solution)/shard_map/all_gather | solution.py:87
  146.9 9.5 %fusion.89 = bf16[256,512]{1,0:T(8,128)(2,1)S(1)} fusion(bf16[1,2,512,8192]{3,2,1,0:T(8,128)(2,1)} %param.9, bf16[1,2,8192,512]{3,2,1,0:T(8,128)(2,1)} %param.10, bf16[2,1,2,1,256,8192]{5,4,3,2,1,0:T(8,128)(2,1)} %param.17, bf16[2,256,512]{2,1,0:T(8,128)(2,1)S(1)} %all_gather.15), kind=kOutput, calls=%fused_computation.61 | convolution fusion | flops 4301389824 | bytes 21495808 | tf_op jit(solution)/shard_map/dot_general | solution.py:50
  156.4 9.5 %fusion.99 = bf16[256,512]{1,0:T(8,128)(2,1)S(1)} fusion(bf16[1,2,512,8192]{3,2,1,0:T(8,128)(2,1)} %param.9, bf16[1,2,8192,512]{3,2,1,0:T(8,128)(2,1)} %param.10, bf16[2,1,2,1,256,8192]{5,4,3,2,1,0:T(8,128)(2,1)} %param.17, bf16[2,256,512]{2,1,0:T(8,128)(2,1)S(1)} %all_gather.15), kind=kOutput, calls=%fused_computation.63 | convolution fusion | flops 4301389824 | bytes 21495808 | tf_op jit(solution)/shard_map/dot_general | solution.py:50
  165.9 1.1 pad_maximum_fusion.1
  167.1 24.8 %reduce-scatter.5.cloned.1.call-done = bf16[64,2048]{1,0:T(8,128)(2,1)} async-done(((bf16[256,2048]{1,0:T(8,128)(2,1)}), bf16[64,2048]{1,0:T(8,128)(2,1)}) %reduce-scatter.5.cloned.1.call-update) | async-done | bytes 262160 | tf_op jit(solution)/shard_map/reduce_scatter | solution.py:100
  191.9 1.0 convert_element_type.177
  192.9 0.2 fusion.146
  193.1 0.2 fusion.159
  193.3 0.7 maximum_bitcast_fusion.1
  194.0 0.7 maximum_bitcast_fusion
  (40 shorter events, 0.8 us)
Async XLA Ops:
  7.2 85.7 %reduce-scatter.3.cloned.1.call-start = ((), (), s32[]{:S(2)}) async-start(), calls=%async_computation.2 | async-start | bytes 1310720 | tf_op jit(solution)/shard_map/reduce_scatter | solution.py:100
  29.1 10.4 %copy-start.2 = (bf16[1,2,1,64,512]{4,3,2,1,0:T(8,128)(2,1)S(1)}, bf16[1,2,1,64,512]{4,3,2,1,0:T(8,128)(2,1)}, u32[]{:S(2)}) copy-start(bf16[1,2,1,64,512]{4,3,2,1,0:T(8,128)(2,1)} %param.13) | copy-start | bytes 393220
  56.4 37.4 %copy-start.1 = (bf16[1,2,1,64,512]{4,3,2,1,0:T(8,128)(2,1)S(1)}, bf16[1,2,1,64,512]{4,3,2,1,0:T(8,128)(2,1)}, u32[]{:S(2)}) copy-start(bf16[1,2,1,64,512]{4,3,2,1,0:T(8,128)(2,1)} %param.12) | copy-start | bytes 393220
  56.5 43.6 %copy-start = (bf16[2,1,2,1,64,512]{5,4,3,2,1,0:T(8,128)(2,1)S(1)}, bf16[2,1,2,1,64,512]{5,4,3,2,1,0:T(8,128)(2,1)}, u32[]{:S(2)}) copy-start(bf16[2,1,2,1,64,512]{5,4,3,2,1,0:T(8,128)(2,1)} %param.16) | copy-start | bytes 786436
  56.5 49.1 %copy-start.4 = (bf16[1,1,64,512]{3,2,1,0:T(8,128)(2,1)S(1)}, bf16[1,1,64,512]{3,2,1,0:T(8,128)(2,1)}, u32[]{:S(2)}) copy-start(bf16[1,1,64,512]{3,2,1,0:T(8,128)(2,1)} %param.14) | copy-start | bytes 196612
  67.1 124.8 %reduce-scatter.5.cloned.1.call-start = ((), (), s32[]{:S(2)}) async-start(), calls=%async_computation.3 | async-start | bytes 1310720 | tf_op jit(solution)/shard_map/reduce_scatter | solution.py:100
  93.9 6.2 %collective-permute-start.1 = (bf16[64,512]{1,0:T(8,128)(2,1)S(1)}, bf16[64,512]{1,0:T(8,128)(2,1)S(1)}, u32[]{:S(2)}, u32[]{:S(2)}) collective-permute-start(bf16[64,512]{1,0:T(8,128)(2,1)S(1)} %fusion.114), channel_id=1, source_target_pairs={{8,0},{16,8},{24,16},{9,1},{17,9},{25,17},{10,2},{18,10},{26,18},{... | collective-permute-start | bytes 196616 | tf_op jit(solution)/shard_map/ppermute | solution.py:16
  100.3 5.3 %collective-permute-start = (bf16[64,512]{1,0:T(8,128)(2,1)S(1)}, bf16[64,512]{1,0:T(8,128)(2,1)S(1)}, u32[]{:S(2)}, u32[]{:S(2)}) collective-permute-start(bf16[64,512]{1,0:T(8,128)(2,1)S(1)} %get-tuple-element.18), channel_id=1, source_target_pairs={{0,8},{8,16},{16,24},{1,9},{9,17},{17,25},{2,10},{10,18},{18,26},{... | collective-permute-start | bytes 196616 | tf_op jit(solution)/shard_map/ppermute | solution.py:16
  112.4 11.7 %collective-permute-start.2 = (bf16[64,512]{1,0:T(8,128)(2,1)S(1)}, bf16[64,512]{1,0:T(8,128)(2,1)S(1)}, u32[]{:S(2)}, u32[]{:S(2)}) collective-permute-start(bf16[64,512]{1,0:T(8,128)(2,1)S(1)} %get-tuple-element.35), channel_id=1, source_target_pairs={{8,0},{16,8},{24,16},{9,1},{17,9},{25,17},{10,2},{18,10},{26,18},{... | collective-permute-start | bytes 196616 | tf_op jit(solution)/shard_map/ppermute | solution.py:16
  124.2 15.7 %copy-start.3 = (bf16[1,1,64,512]{3,2,1,0:T(8,128)(2,1)S(1)}, bf16[1,1,64,512]{3,2,1,0:T(8,128)(2,1)}, u32[]{:S(2)}) copy-start(bf16[1,1,64,512]{3,2,1,0:T(8,128)(2,1)} %param.15) | copy-start | bytes 196612
  124.2 15.7 %collective-permute-start.3 = (bf16[64,512]{1,0:T(8,128)(2,1)S(1)}, bf16[64,512]{1,0:T(8,128)(2,1)S(1)}, u32[]{:S(2)}, u32[]{:S(2)}) collective-permute-start(bf16[64,512]{1,0:T(8,128)(2,1)S(1)} %get-tuple-element.20), channel_id=1, source_target_pairs={{0,8},{8,16},{16,24},{1,9},{9,17},{17,25},{2,10},{10,18},{18,26},{... | collective-permute-start | bytes 196616 | tf_op jit(solution)/shard_map/ppermute | solution.py:16
Sparse Core Ops, SparseCore 0:
  67.3 25.5 reduce-scatter.2
  167.1 24.7 reduce-scatter.4
where the time goes:
time: 202 us
  matrix products  79.5 us (39%)
  waiting for transfers between devices  57.2 us (28%)
  blocking collectives  29.6 us (15%)
  between operations  14.4 us (7%)
  starting transfers between devices  11.3 us (6%)
  other arithmetic  8.82 us (4%)
    reduce_scatter x2, waiting for transfers between devices, body(): lax.psum_scatter(jnp.concatenate([forward_term(gathered[0], weights_in[0,...  50.5 us
    dot_general x4, matrix products, forward_term(): return jnp.dot(hidden, weight_out, preferred_element_type=jnp.float32)  41.6 us
    dot_general x4, matrix products, backward_term(): lax.dot_general(masked, weight_in, contract_last, preferred_element_type=...  37.9 us
    all_gather x2, blocking collectives, body(): lax.all_gather(normed, 'mp', axis=1, tiled=True)  15.2 us
    all_gather x2, blocking collectives, body(): lax.all_gather(grads_now, 'mp', axis=1, tiled=True)  14.5 us
    ppermute x4, starting transfers between devices, from_behind(): lax.ppermute(value, axis, [(source, source + steps) for source in range(l...  11.2 us
    ppermute x4, waiting for transfers between devices, from_behind(): lax.ppermute(value, axis, [(source, source + steps) for source in range(l...  6.61 us
  transfers between devices with their start and end apart: 6, of which 4 were waited for; matrix products, arithmetic and copies ran while one was open for 10% of the time, Pallas kernels for 0%

commit v1 on v0

v1 whole, which is shorter than its diff:
```python
import functools

import jax
import jax.numpy as jnp
from jax import lax
from jax.experimental import pallas as pl
from jax.experimental.pallas import tpu as pltpu
from jax.sharding import PartitionSpec as P

MESH = pl.DeviceIdType.MESH
EPS = 1e-06
TILE = 1024
ORDER = ((True, 0), (False, 0), (False, 1), (True, 1))
F0, B0, B1, F1 = range(4)


def normalize(values, gain_row):
    wide = values.astype(jnp.float32)
    inverse = lax.rsqrt(jnp.mean(wide * wide, axis=-1, keepdims=True) + EPS)
    return (wide * inverse * gain_row).astype(jnp.bfloat16)


def norm_backward(gradient, stashed, gain_row, norm_grad):
    wide = stashed.astype(jnp.float32)
    inverse = lax.rsqrt(jnp.mean(wide * wide, axis=-1, keepdims=True) + EPS)
    scaled = gain_row * norm_grad
    inner = jnp.mean(wide * scaled, axis=-1, keepdims=True)
    result = gradient.astype(jnp.float32) + inverse * scaled - wide * (inverse * inverse * inverse * inner)
    return result.astype(jnp.bfloat16)


def kernel(
    n, sections, ticks, tiles, tile,
    w_in_hbm, w_out_hbm, gains_hbm, acts_hbm, grads_hbm, fresh_a_hbm, fresh_g_hbm, stash_hbm, pre_hbm,
    out_a_hbm, out_g_hbm,
    w_in, w_out, pre, gains, rows_in, fresh, stash,
    gather, acc, s1_send, s1_recv, s2_send, s2_recv, outs, hop,
    w_sem, pre_sem, small_sem, ag_ssem, ag_rsem, s1_ssem, s1_rsem, s2_ssem, s2_rsem, hop_ssem, hop_rsem, out_sem,
):
    me = lax.axis_index("mp")
    seg = lax.axis_index("segment")
    core = lax.rem(me, 2)
    chip = me // 2
    chips = n // 2
    partner = chip * 2 + (1 - core)
    is_first = seg == 0
    is_last = seg == sections - 1
    r = rows_in.shape[2]
    passes = 4 * ticks

    def rows(block):
        return pl.ds(pl.multiple_of(block * r, r), r)

    small = [
        pltpu.make_async_copy(acts_hbm, rows_in.at[0], small_sem.at[0]),
        pltpu.make_async_copy(gains_hbm, gains, small_sem.at[1]),
        pltpu.make_async_copy(grads_hbm, rows_in.at[1], small_sem.at[2]),
        pltpu.make_async_copy(stash_hbm, stash, small_sem.at[3]),
        pltpu.make_async_copy(fresh_a_hbm, fresh.at[0], small_sem.at[4]),
        pltpu.make_async_copy(fresh_g_hbm, fresh.at[1], small_sem.at[5]),
    ]

    def w_copies(leg, i):
        cut = pl.ds(pl.multiple_of(i * tile, tile), tile)
        return (
            pltpu.make_async_copy(w_in_hbm.at[leg, :, cut], w_in.at[leg, i], w_sem.at[0, leg, i]),
            pltpu.make_async_copy(w_out_hbm.at[leg, cut, :], w_out.at[leg, i], w_sem.at[1, leg, i]),
        )

    def pre_copy(t, leg, i):
        cut = pl.ds(pl.multiple_of(i * tile, tile), tile)
        return pltpu.make_async_copy(pre_hbm.at[t, leg, :, cut], pre.at[2 * t + leg, i], pre_sem.at[2 * t + leg, i])

    small[0].start()
    small[1].start()
    small[2].start()
    for i in range(tiles):
        for copy in w_copies(0, i):
            copy.start()
    for copy in small[3:]:
        copy.start()

    barrier = pltpu.get_barrier_semaphore()
    for d in range(1, n):
        pl.semaphore_signal(barrier, inc=1, device_id={"mp": lax.rem(me + d, n)}, device_id_type=MESH)

    @pl.when(seg > 0)
    def _():
        pl.semaphore_signal(barrier, inc=1, device_id={"segment": seg - 1}, device_id_type=MESH)

    @pl.when(seg < sections - 1)
    def _():
        pl.semaphore_signal(barrier, inc=1, device_id={"segment": seg + 1}, device_id_type=MESH)

    peers = n - 1 + (seg > 0).astype(jnp.int32) + (seg < sections - 1).astype(jnp.int32)
    pl.semaphore_wait(barrier, peers)

    def ag_copy(p, d):
        return pltpu.make_async_remote_copy(
            src_ref=gather.at[p, rows(me)], dst_ref=gather.at[p, rows(me)],
            send_sem=ag_ssem.at[p, d - 1], recv_sem=ag_rsem.at[p, d - 1],
            device_id={"mp": lax.rem(me + d, n)}, device_id_type=MESH,
        )

    def s1_copy(p):
        return pltpu.make_async_remote_copy(
            src_ref=s1_send.at[p], dst_ref=s1_recv.at[p],
            send_sem=s1_ssem.at[p], recv_sem=s1_rsem.at[p],
            device_id={"mp": partner}, device_id_type=MESH,
        )

    def s2_copy(p, d):
        return pltpu.make_async_remote_copy(
            src_ref=s2_send.at[p, d - 1], dst_ref=s2_recv.at[p, d - 1],
            send_sem=s2_ssem.at[p, d - 1], recv_sem=s2_rsem.at[p, d - 1],
            device_id={"mp": lax.rem(chip + d, chips) * 2 + core}, device_id_type=MESH,
        )

    def hop_copy(p):
        step = 1 if p % 4 in (F0, B1) else -1
        return pltpu.make_async_remote_copy(
            src_ref=outs.at[p], dst_ref=hop.at[p],
            send_sem=hop_ssem.at[p], recv_sem=hop_rsem.at[p],
            device_id={"segment": seg + step}, device_id_type=MESH,
        )

    def hop_sends(p):
        return jnp.logical_not(is_last) if p % 4 in (F0, B1) else jnp.logical_not(is_first)

    def hop_arrives(p):
        return jnp.logical_not(is_first) if p % 4 in (F0, B1) else jnp.logical_not(is_last)

    def out_copy(p):
        t, (forward, leg) = p // 4, ORDER[p % 4]
        return pltpu.make_async_copy(
            outs.at[p], (out_a_hbm if forward else out_g_hbm).at[t, leg], out_sem.at[p]
        )

    def rows_ref(p):
        forward, leg = ORDER[p % 4]
        return rows_in.at[2 * (p // 4) + (0 if forward else 1), leg]

    def enter(p):
        forward, leg = ORDER[p % 4]
        values = rows_ref(p)[...]
        gather[p, rows(me)] = normalize(values, gains[pl.ds(leg, 1), :]) if forward else values
        for d in range(1, n):
            ag_copy(p, d).start()

    def arrive(p):
        t, kind = p // 4, p % 4
        before = p - 4
        target = rows_ref(p)

        @pl.when(hop_arrives(before))
        def _():
            hop_copy(before).wait_recv()
            target[...] = hop[before]

        @pl.when(jnp.logical_not(hop_arrives(before)))
        def _():
            if kind == F0:
                target[...] = fresh[0, t - 1]
            elif kind == B1:
                target[...] = fresh[1, t - 1]
            elif kind == F1:
                target[...] = outs[before - F1 + F0]
            else:
                target[...] = outs[before - B0 + B1]

        enter(p)

    def scatter_one(p):
        for c in range(chips):
            s1_send[p, c] = acc[p % 2, rows(2 * c + (1 - core))].astype(jnp.bfloat16)
        s1_copy(p).start()

    def scatter_two(p):
        s1_copy(p).wait_recv()
        for d in range(1, chips):
            other = lax.rem(chip + d, chips)
            s2_send[p, d - 1] = (
                acc[p % 2, rows(2 * other + core)] + s1_recv[p, other].astype(jnp.float32)
            ).astype(jnp.bfloat16)
            s2_copy(p, d).start()
        acc[p % 2, rows(me)] += s1_recv[p, chip].astype(jnp.float32)

    def finish(p):
        t, (forward, leg) = p // 4, ORDER[p % 4]
        total = acc[p % 2, rows(me)]
        for d in range(1, chips):
            s2_copy(p, d).wait_recv()
            total = total + s2_recv[p, d - 1].astype(jnp.float32)
        entered = rows_ref(p)[...]
        if forward:
            outs[p] = (entered.astype(jnp.float32) + total).astype(jnp.bfloat16)
        else:
            outs[p] = norm_backward(entered, stash[t, leg], gains[pl.ds(leg, 1), :], total)
        out_copy(p).start()
        if t + 1 < ticks:
            @pl.when(hop_sends(p))
            def _():
                hop_copy(p).start()

    hooks = [[] for _ in range(passes + 1)]

    def at(p, eighth, call):
        hooks[min(p, passes)].append((min(eighth * tiles // 8, tiles - 1), eighth, call))

    at(0, 0, lambda: enter(B0))
    at(0, 4, lambda: (small[3].wait(), small[4].wait(), small[5].wait(), enter(B1)))
    at(1, 0, lambda: enter(F1))
    for p in range(passes):
        at(p + 1, 2, functools.partial(scatter_two, p))
        at(p + 1, 6, functools.partial(finish, p))
    for t in range(1, ticks):
        base = 4 * t
        at(base - 2, 4, functools.partial(arrive, base + F0))
        at(base - 1, 7, functools.partial(arrive, base + B0))
        at(base, 4, functools.partial(arrive, base + B1))
        at(base + 1, 4, functools.partial(arrive, base + F1))
    for entry in hooks:
        entry.sort(key=lambda item: item[1])

    small[0].wait()
    small[1].wait()
    enter(F0)
    small[2].wait()

    for p in range(passes):
        t, (forward, leg) = p // 4, ORDER[p % 4]
        first_use = t == 0 and p % 4 in (F0, B1)
        for d in range(1, n):
            ag_copy(p, d).wait_recv()
        acc[p % 2] = jnp.zeros_like(acc[p % 2])

        def step(i, carry, p=p, t=t, forward=forward, leg=leg, first_use=first_use):
            if p == 0:
                pre_copy(0, 0, i).start()
                for copy in w_copies(1, i):
                    copy.start()
                pre_copy(0, 1, i).start()
            if p % 4 == B0 and t + 1 < ticks:
                pre_copy(t + 1, 0, i).start()
                pre_copy(t + 1, 1, i).start()
            for where, _, call in hooks[p]:
                pl.when(i == where)(lambda call=call: (call(), None)[1])
            if first_use:
                for copy in w_copies(leg, i):
                    copy.wait()
            x = gather[p]
            if forward:
                hidden = jnp.maximum(jnp.dot(x, w_in[leg, i], preferred_element_type=jnp.float32), 0.0)
                acc[p % 2] += jnp.dot(hidden.astype(jnp.bfloat16), w_out[leg, i], preferred_element_type=jnp.float32)
            else:
                pre_copy(t, leg, i).wait()
                up = lax.dot_general(
                    x, w_out[leg, i], (((1,), (1,)), ((), ())), preferred_element_type=jnp.float32
                )
                masked = jnp.where(pre[2 * t + leg, i].astype(jnp.float32) > 0, up, 0.0).astype(jnp.bfloat16)
                acc[p % 2] += lax.dot_general(
                    masked, w_in[leg, i], (((1,), (1,)), ((), ())), preferred_element_type=jnp.float32
                )
            return carry

        lax.fori_loop(0, tiles, step, 0)
        scatter_one(p)

    for _, _, call in hooks[passes]:
        call()

    for p in range(passes):
        for d in range(1, n):
            ag_copy(p, d).wait_send()
        s1_copy(p).wait_send()
        for d in range(1, chips):
            s2_copy(p, d).wait_send()
        if p // 4 + 1 < ticks:
            @pl.when(hop_sends(p))
            def _():
                hop_copy(p).wait_send()
        out_copy(p).wait()


def body(n, sections, w_in, w_out, gains, acts, grads, fresh_a, fresh_g, stash, pre):
    ticks = stash.shape[0]
    _, legs, d, ff = w_in.shape
    r = acts.shape[3]
    total_rows = n * r
    tile = min(TILE, ff)
    tiles = ff // tile
    chips = n // 2
    passes = 4 * ticks
    bf16, f32 = jnp.bfloat16, jnp.float32
    any_spec = pl.BlockSpec(memory_space=pl.ANY)
    dma = pltpu.SemaphoreType.DMA
    far = max(chips - 1, 1)
    out = jax.ShapeDtypeStruct((ticks, legs, r, d), bf16)
    out_a, out_g = pl.pallas_call(
        functools.partial(kernel, n, sections, ticks, tiles, tile),
        out_shape=(out, out),
        in_specs=[any_spec] * 9,
        out_specs=(any_spec, any_spec),
        scratch_shapes=[
            pltpu.VMEM((legs, tiles, d, tile), bf16),
            pltpu.VMEM((legs, tiles, tile, d), bf16),
            pltpu.VMEM((ticks * legs, tiles, total_rows, tile), bf16),
            pltpu.VMEM((legs, d), f32),
            pltpu.VMEM((2 * ticks, legs, r, d), bf16),
            pltpu.VMEM((2,) + (max(ticks - 1, 1), r, d), bf16),
            pltpu.VMEM((ticks, legs, r, d), bf16),
            pltpu.VMEM((passes, total_rows, d), bf16),
            pltpu.VMEM((2, total_rows, d), f32),
            pltpu.VMEM((passes, chips, r, d), bf16),
            pltpu.VMEM((passes, chips, r, d), bf16),
            pltpu.VMEM((passes, far, r, d), bf16),
            pltpu.VMEM((passes, far, r, d), bf16),
            pltpu.VMEM((passes, r, d), bf16),
            pltpu.VMEM((passes, r, d), bf16),
            dma((2, legs, tiles)),
            dma((ticks * legs, tiles)),
            dma((6,)),
            dma((passes, n - 1)),
            dma((passes, n - 1)),
            dma((passes,)),
            dma((passes,)),
            dma((passes, far)),
            dma((passes, far)),
            dma((passes,)),
            dma((passes,)),
            dma((passes,)),
        ],
        compiler_params=pltpu.CompilerParams(
            collective_id=0, has_side_effects=True, vmem_limit_bytes=67043328
        ),
        name="relay",
    )(
        w_in[0], w_out[0], gains[0], acts[0, :, 0], grads[0, :, 0],
        fresh_a[:, 0], fresh_g[:, 0], stash[:, 0, :, 0], pre[:, 0, :, 0],
    )
    return out_a[:, None, :, None], out_g[:, None, :, None]


def solution(mesh):
    return jax.shard_map(
        functools.partial(body, mesh.shape["mp"], mesh.shape["segment"]),
        mesh=mesh,
        in_specs=(
            P("segment", None, None, "mp"),
            P("segment", None, "mp", None),
            P("segment", None, None),
            P("segment", None, "tok", "mp", None),
            P("segment", None, "tok", "mp", None),
            P(None, "tok", "mp", None),
            P(None, "tok", "mp", None),
            P(None, "segment", None, "tok", "mp", None),
            P(None, "segment", None, "tok", None, "mp"),
        ),
        out_specs=(
            P(None, "segment", None, "tok", "mp", None),
            P(None, "segment", None, "tok", "mp", None),
        ),
        check_vma=False,
    )
```

time: 202 us -> 73.2 us (0.36)
  matrix products: 79.5 us -> 0 us
  Pallas kernels: 0 us -> 69.1 us
  waiting for transfers between devices: 57.2 us -> 0 us
  blocking collectives: 29.6 us -> 0 us
  between operations: 14.4 us -> 0.64 us
  starting transfers between devices: 11.3 us -> 0 us
  other arithmetic: 8.82 us -> 0 us
  local copies, waits for them, and re-layouts: 0.8 us -> 3.34 us
    dot_general x8 -> x0, matrix products: 79.5 us -> none  [the longest x4 41.6 us: forward_term(): return jnp.dot(hidden, weight_out, preferred_element_type=jnp.float32)]
    pallas_call x0 -> x1, Pallas kernels: none -> 69.1 us  [body(): pl.pallas_call(functools.partial(kernel, n, sections, ticks, tiles, tile)...]
    reduce_scatter x2 -> x0, waiting for transfers between devices: 50.5 us -> none  [body(): lax.psum_scatter(jnp.concatenate([forward_term(gathered[0], weights_in[0,...]
    all_gather x4 -> x0, blocking collectives: 29.6 us -> none  [the longest x2 15.2 us: body(): lax.all_gather(normed, 'mp', axis=1, tiled=True)]
    ppermute x4 -> x0, starting transfers between devices: 11.2 us -> none  [from_behind(): lax.ppermute(value, axis, [(source, source + steps) for source in range(l...]
    ppermute x4 -> x0, waiting for transfers between devices: 6.61 us -> none  [from_behind(): lax.ppermute(value, axis, [(source, source + steps) for source in range(l...]
    unnamed x10 -> x2, local copies, waits for them, and re-layouts: 0.03 us -> 3.34 us
    concatenate x2 -> x0, other arithmetic: 2.23 us -> none  [body(): jnp.concatenate([forward_term(gathered[0], weights_in[0, 0], weights_out[...]
  transfers between devices with their start and end apart: 6 -> 0, of which waited for: 4 -> 0; matrix products, arithmetic and copies ran while one was open for 10% -> 0% of each run, Pallas kernels for 0% -> 0%
where the time goes in v1:
time: 73.2 us; the launch traced here: 73.1 us
  Pallas kernels  69.1 us (94%)
  local copies, waits for them, and re-layouts  3.34 us (5%)
    pallas_call x1, Pallas kernels, body(): pl.pallas_call(functools.partial(kernel, n, sections, ticks, tiles, tile)...  69.1 us
    unnamed x2, local copies, waits for them, and re-layouts  3.34 us

profile of v1, /device:TPU:0, one launch (start us, length us, event | category | flops | bytes accessed | tf_op | source)
XLA Modules:
  0.0 73.1 jit_solution(3260218221052487104)
XLA Ops:
  0.6 69.1 %relay.1 = (bf16[2,2,64,512]{3,2,1,0:T(8,128)(2,1)}, bf16[2,2,64,512]{3,2,1,0:T(8,128)(2,1)}) custom-call(bf16[2,512,8192]{2,1,0:T(8,128)(2,1)} %bitcast.15, bf16[2,8192,512]{2,1,0:T(8,128)(2,1)} %bitcast.16, f32[2,512]{1,0:T(2,128)} %bitcast.25, bf16[2,64,512]{2,1,0:T(8,128)(2,1)} %bitcast.21, bf16[2,64,512]{2,1,0:T(8,128)(2,1)} %bitcast.22, ...), custom_call_target="tpu_custom_call" | custom-call | tf_op jit(solution)/shard_map/relay/pallas_call | solution.py:299
  69.7 1.7 %copy.15 = bf16[2,1,2,1,64,512]{5,4,3,2,1,0:T(8,128)(2,1)} copy(bf16[2,1,2,1,64,512]{5,4,3,2,1,0:T(8,128)(2,1)} %bitcast.20) | data formatting | bytes 524288
  71.4 1.7 %copy.16 = bf16[2,1,2,1,64,512]{5,4,3,2,1,0:T(8,128)(2,1)} copy(bf16[2,1,2,1,64,512]{5,4,3,2,1,0:T(8,128)(2,1)} %bitcast.19) | data formatting | bytes 524288

commit v2 on v1

--- a/solution.py
+++ b/solution.py
@@ -9,7 +9,10 @@
 
 MESH = pl.DeviceIdType.MESH
 EPS = 1e-06
-TILE = 1024
+TILE = 2048
+S_TWO = 2
+S_FIN = 8
+ARRIVE = (22, 32, 38, 46)
 ORDER = ((True, 0), (False, 0), (False, 1), (True, 1))
 F0, B0, B1, F1 = range(4)
 
@@ -34,8 +37,8 @@
     w_in_hbm, w_out_hbm, gains_hbm, acts_hbm, grads_hbm, fresh_a_hbm, fresh_g_hbm, stash_hbm, pre_hbm,
     out_a_hbm, out_g_hbm,
     w_in, w_out, pre, gains, rows_in, fresh, stash,
-    gather, acc, s1_send, s1_recv, s2_send, s2_recv, outs, hop,
-    w_sem, pre_sem, small_sem, ag_ssem, ag_rsem, s1_ssem, s1_rsem, s2_ssem, s2_rsem, hop_ssem, hop_rsem, out_sem,
+    gather, acc, own, s1_send, s1_recv, s2_send, s2_recv, outs, hop,
+    w_sem, pre_sem, small_sem, far_ssem, far_rsem, near_ssem, near_rsem, s1_ssem, s1_rsem, s2_ssem, s2_rsem, hop_ssem, hop_rsem, out_sem,
 ):
     me = lax.axis_index("mp")
     seg = lax.axis_index("segment")
@@ -74,9 +77,8 @@
     small[0].start()
     small[1].start()
     small[2].start()
-    for i in range(tiles):
-        for copy in w_copies(0, i):
-            copy.start()
+    for copy in w_copies(0, 0):
+        copy.start()
     for copy in small[3:]:
         copy.start()
 
@@ -95,11 +97,19 @@
     peers = n - 1 + (seg > 0).astype(jnp.int32) + (seg < sections - 1).astype(jnp.int32)
     pl.semaphore_wait(barrier, peers)
 
-    def ag_copy(p, d):
+    def far_copy(p, d):
         return pltpu.make_async_remote_copy(
             src_ref=gather.at[p, rows(me)], dst_ref=gather.at[p, rows(me)],
-            send_sem=ag_ssem.at[p, d - 1], recv_sem=ag_rsem.at[p, d - 1],
-            device_id={"mp": lax.rem(me + d, n)}, device_id_type=MESH,
+            send_sem=far_ssem.at[p, d - 1], recv_sem=far_rsem.at[p, d - 1],
+            device_id={"mp": lax.rem(chip + d, chips) * 2 + core}, device_id_type=MESH,
+        )
+
+    def near_copy(p, d):
+        block = lax.rem(chip + chips - d, chips) * 2 + core
+        return pltpu.make_async_remote_copy(
+            src_ref=gather.at[p, rows(block)], dst_ref=gather.at[p, rows(block)],
+            send_sem=near_ssem.at[p, d], recv_sem=near_rsem.at[p, d],
+            device_id={"mp": partner}, device_id_type=MESH,
         )
 
     def s1_copy(p):
@@ -144,8 +154,14 @@
         forward, leg = ORDER[p % 4]
         values = rows_ref(p)[...]
         gather[p, rows(me)] = normalize(values, gains[pl.ds(leg, 1), :]) if forward else values
-        for d in range(1, n):
-            ag_copy(p, d).start()
+        for d in range(1, chips):
+            far_copy(p, d).start()
+        near_copy(p, 0).start()
+
+    def relay(p):
+        for d in range(1, chips):
+            far_copy(p, d).wait_recv()
+            near_copy(p, d).start()
 
     def arrive(p):
         t, kind = p // 4, p % 4
@@ -183,11 +199,11 @@
                 acc[p % 2, rows(2 * other + core)] + s1_recv[p, other].astype(jnp.float32)
             ).astype(jnp.bfloat16)
             s2_copy(p, d).start()
-        acc[p % 2, rows(me)] += s1_recv[p, chip].astype(jnp.float32)
+        own[p] = acc[p % 2, rows(me)] + s1_recv[p, chip].astype(jnp.float32)
 
     def finish(p):
         t, (forward, leg) = p // 4, ORDER[p % 4]
-        total = acc[p % 2, rows(me)]
+        total = own[p]
         for d in range(1, chips):
             s2_copy(p, d).wait_recv()
             total = total + s2_recv[p, d - 1].astype(jnp.float32)
@@ -203,43 +219,53 @@
                 hop_copy(p).start()
 
     hooks = [[] for _ in range(passes + 1)]
+    order = []
 
     def at(p, eighth, call):
-        hooks[min(p, passes)].append((min(eighth * tiles // 8, tiles - 1), eighth, call))
-
-    at(0, 0, lambda: enter(B0))
+        key = (8 * p + eighth, len(order))
+        order.append(key)
+        hooks[min(p, passes)].append((min(eighth * tiles // 8, tiles - 1), key, call))
+
     at(0, 4, lambda: (small[3].wait(), small[4].wait(), small[5].wait(), enter(B1)))
+    at(0, 6, lambda: relay(B0))
     at(1, 0, lambda: enter(F1))
+    at(1, 2, lambda: relay(B1))
+    at(1, 6, lambda: relay(F1))
     for p in range(passes):
-        at(p + 1, 2, functools.partial(scatter_two, p))
-        at(p + 1, 6, functools.partial(finish, p))
+        at(p + 1, S_TWO, functools.partial(scatter_two, p))
+        at(p + 1 + S_FIN // 8, S_FIN % 8, functools.partial(finish, p))
     for t in range(1, ticks):
-        base = 4 * t
-        at(base - 2, 4, functools.partial(arrive, base + F0))
-        at(base - 1, 7, functools.partial(arrive, base + B0))
-        at(base, 4, functools.partial(arrive, base + B1))
-        at(base + 1, 4, functools.partial(arrive, base + F1))
+        for kind in range(4):
+            slot = ARRIVE[kind]
+            at(4 * t - 4 + slot // 8, slot % 8, functools.partial(arrive, 4 * t + kind))
+            at(4 * t - 4 + (slot + 6) // 8, (slot + 6) % 8, functools.partial(relay, 4 * t + kind))
     for entry in hooks:
         entry.sort(key=lambda item: item[1])
 
     small[0].wait()
     small[1].wait()
     enter(F0)
+    for i in range(1, tiles):
+        for copy in w_copies(0, i):
+            copy.start()
+    for i in range(tiles):
+        pre_copy(0, 0, i).start()
+    for i in range(tiles):
+        pre_copy(0, 1, i).start()
+        for copy in w_copies(1, i):
+            copy.start()
+    relay(F0)
     small[2].wait()
+    enter(B0)
 
     for p in range(passes):
         t, (forward, leg) = p // 4, ORDER[p % 4]
         first_use = t == 0 and p % 4 in (F0, B1)
-        for d in range(1, n):
-            ag_copy(p, d).wait_recv()
+        for d in range(chips):
+            near_copy(p, d).wait_recv()
         acc[p % 2] = jnp.zeros_like(acc[p % 2])
 
         def step(i, carry, p=p, t=t, forward=forward, leg=leg, first_use=first_use):
-            if p == 0:
-                pre_copy(0, 0, i).start()
-                for copy in w_copies(1, i):
-                    copy.start()
-                pre_copy(0, 1, i).start()
             if p % 4 == B0 and t + 1 < ticks:
                 pre_copy(t + 1, 0, i).start()
                 pre_copy(t + 1, 1, i).start()
@@ -270,8 +296,10 @@
         call()
 
     for p in range(passes):
-        for d in range(1, n):
-            ag_copy(p, d).wait_send()
+        for d in range(1, chips):
+            far_copy(p, d).wait_send()
+        for d in range(chips):
+            near_copy(p, d).wait_send()
         s1_copy(p).wait_send()
         for d in range(1, chips):
             s2_copy(p, d).wait_send()
@@ -280,6 +308,19 @@
             def _():
                 hop_copy(p).wait_send()
         out_copy(p).wait()
+
+
+def flush(a_ref, g_ref, out_a_ref, out_g_ref, held, sem):
+    pairs = ((a_ref, out_a_ref), (g_ref, out_g_ref))
+    loads = [pltpu.make_async_copy(src, held.at[k], sem.at[0, k]) for k, (src, _) in enumerate(pairs)]
+    stores = [pltpu.make_async_copy(held.at[k], dst, sem.at[1, k]) for k, (_, dst) in enumerate(pairs)]
+    for copy in loads:
+        copy.start()
+    for load, store in zip(loads, stores):
+        load.wait()
+        store.start()
+    for copy in stores:
+        copy.wait()
 
 
 def body(n, sections, w_in, w_out, gains, acts, grads, fresh_a, fresh_g, stash, pre):
@@ -311,6 +352,7 @@
             pltpu.VMEM((ticks, legs, r, d), bf16),
             pltpu.VMEM((passes, total_rows, d), bf16),
             pltpu.VMEM((2, total_rows, d), f32),
+            pltpu.VMEM((passes, r, d), f32),
             pltpu.VMEM((passes, chips, r, d), bf16),
             pltpu.VMEM((passes, chips, r, d), bf16),
             pltpu.VMEM((passes, far, r, d), bf16),
@@ -320,8 +362,10 @@
             dma((2, legs, tiles)),
             dma((ticks * legs, tiles)),
             dma((6,)),
-            dma((passes, n - 1)),
-            dma((passes, n - 1)),
+            dma((passes, far)),
+            dma((passes, far)),
+            dma((passes, chips)),
+            dma((passes, chips)),
             dma((passes,)),
             dma((passes,)),
             dma((passes, far)),
@@ -338,6 +382,14 @@
         w_in[0], w_out[0], gains[0], acts[0, :, 0], grads[0, :, 0],
         fresh_a[:, 0], fresh_g[:, 0], stash[:, 0, :, 0], pre[:, 0, :, 0],
     )
+    out_a, out_g = pl.pallas_call(
+        flush,
+        out_shape=(out, out),
+        in_specs=[any_spec] * 2,
+        out_specs=(any_spec, any_spec),
+        scratch_shapes=[pltpu.VMEM((2,) + out.shape, bf16), dma((2, 2))],
+        name="flush",
+    )(out_a, out_g)
     return out_a[:, None, :, None], out_g[:, None, :, None]
 
 

time: 73.2 us -> 59.8 us (0.82)
  Pallas kernels: 69.1 us -> 59 us
  local copies, waits for them, and re-layouts: 3.34 us -> 0 us
    pallas_call x1, Pallas kernels: 69.1 us -> 57.2 us  [body(): pl.pallas_call(functools.partial(kernel, n, sections, ticks, tiles, tile)...]
    unnamed x2 -> x0, local copies, waits for them, and re-layouts: 3.34 us -> none
    pallas_call x0 -> x1, Pallas kernels: none -> 1.77 us  [body(): pl.pallas_call(flush, out_shape=(out, out), in_specs=[any_spec] * 2, out_...]
where the time goes in v2:
time: 59.8 us; the launch traced here: 59.6 us
  Pallas kernels  59 us (99%)
  between operations  0.64 us (1%)
    pallas_call x1, Pallas kernels, body(): pl.pallas_call(functools.partial(kernel, n, sections, ticks, tiles, tile)...  57.2 us
    pallas_call x1, Pallas kernels, body(): pl.pallas_call(flush, out_shape=(out, out), in_specs=[any_spec] * 2, out_...  1.77 us

profile of v2, /device:TPU:0, one launch (start us, length us, event | category | flops | bytes accessed | tf_op | source)
XLA Modules:
  0.0 59.6 jit_solution(17608896605056367800)
XLA Ops:
  0.6 57.2 %relay.1 = (bf16[2,2,64,512]{3,2,1,0:T(8,128)(2,1)}, bf16[2,2,64,512]{3,2,1,0:T(8,128)(2,1)}) custom-call(bf16[2,512,8192]{2,1,0:T(8,128)(2,1)} %bitcast.15, bf16[2,8192,512]{2,1,0:T(8,128)(2,1)} %bitcast.16, f32[2,512]{1,0:T(2,128)} %bitcast.23, bf16[2,64,512]{2,1,0:T(8,128)(2,1)} %bitcast.19, bf16[2,64,512]{2,1,0:T(8,128)(2,1)} %bitcast.20, ...), custom_call_target="tpu_custom_call" | custom-call | tf_op jit(solution)/shard_map/relay/pallas_call | solution.py:340
  57.8 1.8 %flush.1 = (bf16[2,2,64,512]{3,2,1,0:T(8,128)(2,1)}, bf16[2,2,64,512]{3,2,1,0:T(8,128)(2,1)}) custom-call(bf16[2,2,64,512]{3,2,1,0:T(8,128)(2,1)} %get-tuple-element.6.a_ref, bf16[2,2,64,512]{3,2,1,0:T(8,128)(2,1)} %get-tuple-element.7.g_ref), custom_call_target="tpu_custom_call" | custom-call | tf_op jit(solution)/shard_map/flush/pallas_call | solution.py:385
